TPU v7x, 32 devices: a whole 2x2x4 slice. The times are simulated.
32 devices in a mesh: dom: 16 (over z, x, core), col: 2 (over y).
Axes of the slice: x: 2, y: 2, z: 4, core: 2. Of those that a mesh axis runs over, the one named last changes fastest.
Arguments:
- feats: bfloat16 [8192, 256], P('dom', 'col'), may hold values from -6 to 6
- w_first: bfloat16 [256, 256], replicated, may hold values from -0.375 to 0.375
- w_second: bfloat16 [256, 256], replicated, may hold values from -0.375 to 0.375
- block_cols: int32 [64, 32], P('dom'), may hold values from 0 to 63, as said below
- block_count: int32 [64], P('dom'), may hold values from 1 to 32
- block_vals: bfloat16 [64, 32, 128, 128], P('dom', 'col'), may hold values from -0.125 to 0.125
- cotangent: bfloat16 [8192, 256], P('dom', 'col'), may hold values from -6 to 6
Outputs:
- output: float32 [8192, 256], P('dom', 'col')
- grad_first: float32 [256, 256], P(None, 'col')
- grad_second: float32 [256, 256], P(None, 'col')
Inputs may be any that keep to these rules, and one draw needn't show every extreme that they name: Each row of block_cols names 32 different column blocks.
All inputs are finite; a program needn't handle non-finite values.
Results may differ from a plain program's by a relative error of at most 0.019.
Values may be sent and summed in bfloat16 or wider, within the bound.
No kernel may reach another device: no remote copies, remote signals or barrier semaphores. Data moves between devices by JAX's collectives and lax.ppermute only.
A program may use at most 64 MiB of HBM per device.

v0:
```python
import jax
import jax.numpy as jnp
from jax import lax
from jax.sharding import PartitionSpec as P

BLK = 128


def silu_slope(value):
    sig = jax.nn.sigmoid(value)
    return sig + value * sig * (1.0 - sig)


def forward_fold(prod, cols, vals):
    rows, width = prod.shape
    piece = lax.all_gather(prod, "dom", axis=0, tiled=True)
    count_blocks = piece.shape[0] // BLK
    hit = (cols >= 0) & (cols < count_blocks)
    picked = piece.reshape(count_blocks, BLK, width)[jnp.clip(cols, 0, count_blocks - 1)]
    picked = jnp.where(hit[:, :, None, None], picked, jnp.zeros((), picked.dtype))
    contrib = jnp.einsum("rkij,rkjf->rif", vals, picked, preferred_element_type=jnp.float32)
    return contrib.reshape(rows, width)


def backward_scatter(grad, cols, vals):
    rows, width = grad.shape
    nblocks = rows // BLK
    products = jnp.einsum(
        "rkij,rif->rkjf",
        vals,
        grad.reshape(nblocks, BLK, width),
        preferred_element_type=jnp.float32,
    )
    count = rows * lax.axis_size("dom")
    count_blocks = count // BLK
    onehot = (cols[:, :, None] == jnp.arange(count_blocks)[None, None, :]).astype(jnp.float32)
    summed = jnp.einsum("rkp,rkjf->pjf", onehot, products, precision=lax.Precision.HIGHEST)
    return lax.psum_scatter(summed.reshape(count, width), "dom", scatter_dimension=0, tiled=True)


def body(feats, w_first, w_second, block_cols, block_count, block_vals, cotangent):
    col_index = lax.axis_index("col")
    rows, narrow = feats.shape

    def widen(value):
        return lax.all_gather(value, "col", axis=1, tiled=True)

    def weight_grad(full, back):
        return lax.psum(
            jnp.dot(full.T, back, preferred_element_type=jnp.float32).astype(jnp.bfloat16), "dom"
        ).astype(jnp.float32)

    all_vals = lax.all_gather(block_vals, "col", axis=1, tiled=True)
    slot_ids = jnp.arange(all_vals.shape[1])
    usable = slot_ids[None, :] < block_count[:, None]
    vals = jnp.where(usable[:, :, None, None], all_vals, jnp.zeros((), all_vals.dtype))

    def project(full, weight):
        weight_cols = lax.dynamic_slice_in_dim(weight, col_index * narrow, narrow, 1)
        return jnp.dot(full, weight_cols, preferred_element_type=jnp.float32).astype(jnp.bfloat16)

    def aggregate(prod):
        return forward_fold(prod, block_cols, vals)

    def transpose(grad):
        return backward_scatter(grad, block_cols, vals)

    full_input = widen(feats)
    first = aggregate(project(full_input, w_first))
    hidden = (first * jax.nn.sigmoid(first)).astype(jnp.bfloat16)
    full_hidden = widen(hidden)
    output = aggregate(project(full_hidden, w_second))
    back_second = transpose(cotangent).astype(jnp.bfloat16)
    grad_second = weight_grad(full_hidden, back_second)
    second_cols = lax.dynamic_slice_in_dim(w_second, col_index * narrow, narrow, 1)
    partial_hidden = jnp.dot(back_second, second_cols.T, preferred_element_type=jnp.float32)
    hidden_grad = lax.psum_scatter(partial_hidden, "col", scatter_dimension=1, tiled=True)
    act_grad = (hidden_grad * silu_slope(first)).astype(jnp.bfloat16)
    back_first = transpose(act_grad).astype(jnp.bfloat16)
    grad_first = weight_grad(full_input, back_first)
    return (output, grad_first, grad_second)


def solution(mesh):
    in_specs = (
        P("dom", "col"),
        P(),
        P(),
        P("dom", None),
        P("dom"),
        P("dom", "col", None, None),
        P("dom", "col"),
    )
    out_specs = (P("dom", "col"), P(None, "col"), P(None, "col"))
    return jax.shard_map(body, mesh=mesh, in_specs=in_specs, out_specs=out_specs, check_vma=False)
```

profile of v0, /device:TPU:8, one launch (start us, length us, event | category | flops | bytes accessed | tf_op | source)
XLA Modules:
  0.0 452.0 jit_solution(4109258928189561779)
XLA Ops:
  7.2 0.0 all-gather.4.cloned.1.call-start
  7.2 0.7 all-gather.4.cloned.1.call-update
  7.9 0.0 reduce-scatter.4.cloned.1.call-start
  8.0 0.7 iota_compare_fusion.1
  8.7 58.8 %all-gather.4.cloned.1.call-done = bf16[4,32,128,128]{3,2,1,0:T(8,128)(2,1)} async-done(((bf16[4,16,128,128]{3,2,1,0:T(8,128)(2,1)}), bf16[4,32,128,128]{3,2,1,0:T(8,128)(2,1)}) %all-gather.4.cloned.1.call-update) | async-done | bytes 4194320 | tf_op jit(solution)/shard_map/all_gather | solution.py:53
  67.4 4.5 broadcast_select_fusion
  71.9 7.9 %copy.18 = bf16[4,32,128,128]{2,1,0,3:T(8,128)(2,1)} copy(bf16[4,32,128,128]{3,2,1,0:T(8,128)(2,1)} %broadcast_select_fusion) | data formatting | bytes 8388608 | tf_op jit(solution)/shard_map/jit(_where)/select_n | solution.py:56
  79.9 3.4 fusion.31
  83.3 3.9 convolution_bitcast_fusion.1
  87.3 4.4 copy.13
  91.7 0.0 reduce-scatter.4.cloned.1.call-update
  91.7 0.0 all-gather.6.cloned.1.call-start
  91.8 0.8 copy-done.2
  92.6 5.8 %all_gather.16 = bf16[512,256]{1,0:T(8,128)(2,1)S(1)} all-gather(bf16[512,128]{1,0:T(8,128)(2,1)S(1)} %copy-done.2), channel_id=1, replica_groups=mesh['dom'=16,'col'=2] {'col'}, dimensions={1}, use_global_device_ids=true | all-gather | bytes 393216 | tf_op jit(solution)/shard_map/all_gather | solution.py:46
  98.4 0.9 fusion.8
  99.3 0.0 all-gather.6.cloned.1.call-update
  99.3 0.0 reduce-scatter.6.cloned.1.call-start
  99.3 64.6 %reduce-scatter.4.cloned.1.call-done = f32[512,128]{1,0:T(8,128)} async-done(((f32[8192,128]{1,0:T(8,128)}), f32[512,128]{1,0:T(8,128)}) %reduce-scatter.4.cloned.1.call-update) | async-done | bytes 262160 | tf_op jit(solution)/shard_map/reduce_scatter | solution.py:38
  163.9 2.0 fusion.16
  165.9 0.0 reduce-scatter.6.cloned.1.call-update
  165.9 0.0 all-gather.8.cloned.1.call-start
  166.0 0.1 reshape.63
  166.1 40.7 %all-gather.6.cloned.1.call-done = bf16[8192,128]{0,1:T(8,128)(2,1)} async-done(((bf16[512,128]{0,1:T(8,128)(2,1)}), bf16[8192,128]{0,1:T(8,128)(2,1)}) %all-gather.6.cloned.1.call-update) | async-done | bytes 2097168 | tf_op jit(solution)/shard_map/all_gather | solution.py:16
  206.8 3.2 copy.21
  210.0 3.0 gather_fusion
  213.0 5.0 %fusion.2 = f32[4,128,128,1]{2,1,3,0:T(8,128)S(1)} fusion(bf16[4,32,128,128]{3,2,1,0:T(8,128)(2,1)} %broadcast_select_fusion, bf16[4,32,128,128]{3,2,1,0:T(8,128)(2,1)} %bitcast.68, pred[4,32]{1,0:T(4,128)(4,1)S(1)} %compare_and_fusion), kind=kOutput, calls=%fused_computation.4 | convolution fusion | flops 538968064 | bytes 8650880 | tf_op jit(solution)/shard_map/rkij,rkjf->rif/dot_general | solution.py:21
  218.0 5.3 %reduce-scatter.6.cloned.1.call-done = f32[512,128]{1,0:T(8,128)} async-done(((f32[512,256]{1,0:T(8,128)}), f32[512,128]{1,0:T(8,128)}) %reduce-scatter.6.cloned.1.call-update) | async-done | bytes 262160 | tf_op jit(solution)/shard_map/reduce_scatter | solution.py:77
  223.3 1.1 multiply_convert_fusion
  224.4 5.8 %all_gather.18 = bf16[512,256]{1,0:T(8,128)(2,1)S(1)} all-gather(bf16[512,128]{1,0:T(8,128)(2,1)S(1)} %get-tuple-element.12), channel_id=1, replica_groups=mesh['dom'=16,'col'=2] {'col'}, dimensions={1}, use_global_device_ids=true | all-gather | bytes 393216 | tf_op jit(solution)/shard_map/all_gather | solution.py:46
  230.2 0.9 convolution_convert_fusion
  231.1 0.0 all-gather.8.cloned.1.call-update
  231.1 0.2 reduce-scatter.8.cloned.1.call-start
  231.3 3.4 fusion.32
  234.8 3.9 convolution_bitcast_fusion
  238.7 4.4 copy.14
  243.1 0.0 reduce-scatter.8.cloned.1.call-update
  243.1 0.0 all-reduce.3.cloned.1.call-start
  243.2 0.9 copy-done.1
  244.1 0.9 convolution_convert_fusion.2
  245.0 26.6 %all-gather.8.cloned.1.call-done = bf16[8192,128]{1,0:T(8,128)(2,1)} async-done(((bf16[512,128]{1,0:T(8,128)(2,1)}), bf16[8192,128]{1,0:T(8,128)(2,1)}) %all-gather.8.cloned.1.call-update) | async-done | bytes 2097168 | tf_op jit(solution)/shard_map/all_gather | solution.py:16
  271.6 4.7 %gather_fusion.1 = bf16[128,128,128]{2,1,0:T(8,128)(2,1)} fusion(bf16[64,128,128]{2,1,0:T(8,128)(2,1)} %bitcast.66, s32[1024]{0:T(1024)S(1)} %pad_clamp_fusion), kind=kCustom, calls=%fused_computation.1 | custom fusion | bytes 8389120 | tf_op jit(solution)/shard_map/gather | solution.py:19
  276.2 71.0 %reduce-scatter.8.cloned.1.call-done = f32[512,128]{1,0:T(8,128)} async-done(((f32[8192,128]{1,0:T(8,128)}), f32[512,128]{1,0:T(8,128)}) %reduce-scatter.8.cloned.1.call-update) | async-done | bytes 262160 | tf_op jit(solution)/shard_map/reduce_scatter | solution.py:38
  347.3 1.8 fusion.9
  349.1 0.0 all-reduce.3.cloned.1.call-update
  349.1 5.5 %fusion = f32[4,128,128,1]{2,1,3,0:T(8,128)} fusion(bf16[4,32,128,128]{3,2,1,0:T(8,128)(2,1)} %broadcast_select_fusion, bf16[4,32,128,128]{3,2,1,0:T(8,128)(2,1)} %bitcast.67, pred[4,32]{1,0:T(4,128)(4,1)S(1)} %compare_and_fusion), kind=kOutput, calls=%fused_computation.2 | convolution fusion | flops 538968064 | bytes 8650880 | tf_op jit(solution)/shard_map/rkij,rkjf->rif/dot_general | solution.py:21
  354.6 87.5 %all-reduce.3.cloned.1.call-done = (bf16[256,128]{0,1:T(8,128)(2,1)}, bf16[256,128]{1,0:T(8,128)(2,1)}) async-done(((bf16[256,128]{0,1:T(8,128)(2,1)}, bf16[256,128]{1,0:T(8,128)(2,1)}), (bf16[256,128]{0,1:T(8,128)(2,1)}, bf16[256,128]{1,0:T(8,128)(2,1)})) %all-reduce.3.cloned.1.call-update) | async-done | bytes 131088 | tf_op jit(solution)/shard_map/psum | solution.py:49
  442.1 1.6 copy.15
  443.7 1.5 convert_element_type.49
  (13 shorter events, 0.0 us)
Async XLA Ops:
  7.2 72.7 %copy-start = (bf16[512,128]{1,0:T(8,128)(2,1)S(1)}, bf16[512,128]{1,0:T(8,128)(2,1)}, u32[]{:S(2)}) copy-start(bf16[512,128]{1,0:T(8,128)(2,1)} %param.13) | copy-start | bytes 393220
  7.2 60.3 %all-gather.4.cloned.1.call-start = ((), (), s32[]{:S(2)}) async-start(), calls=%async_computation.3 | async-start | bytes 6291456 | tf_op jit(solution)/shard_map/all_gather | solution.py:53
  7.9 156.0 %reduce-scatter.4.cloned.1.call-start = ((), (), s32[]{:S(2)}) async-start(), calls=%async_computation.6 | async-start | bytes 4456448 | tf_op jit(solution)/shard_map/reduce_scatter | solution.py:38
  79.9 3.4 copy-start.5
  91.7 0.9 copy-start.2
  91.7 6.7 %copy-start.4 = (bf16[256,256]{1,0:T(8,128)(2,1)S(1)}, bf16[256,256]{1,0:T(8,128)(2,1)}, u32[]{:S(2)}) copy-start(bf16[256,256]{1,0:T(8,128)(2,1)} %param.8) | copy-start | bytes 393220
  91.7 72.2 %copy-start.3 = (bf16[256,256]{1,0:T(8,128)(2,1)S(1)}, bf16[256,256]{1,0:T(8,128)(2,1)}, u32[]{:S(2)}) copy-start(bf16[256,256]{1,0:T(8,128)(2,1)} %param.9) | copy-start | bytes 393220
  91.7 115.1 %all-gather.6.cloned.1.call-start = ((), (), s32[]{:S(2)}) async-start(), calls=%async_computation.4 | async-start | bytes 2228224 | tf_op jit(solution)/shard_map/all_gather | solution.py:16
  99.3 124.0 %reduce-scatter.6.cloned.1.call-start = ((), (), s32[]{:S(2)}) async-start(), calls=%async_computation.7 | async-start | bytes 786432 | tf_op jit(solution)/shard_map/reduce_scatter | solution.py:77
  165.9 105.6 %all-gather.8.cloned.1.call-start = ((), (), s32[]{:S(2)}) async-start(), calls=%async_computation.5 | async-start | bytes 2228224 | tf_op jit(solution)/shard_map/all_gather | solution.py:16
  231.1 116.2 %reduce-scatter.8.cloned.1.call-start = ((), (), s32[]{:S(2)}) async-start(), calls=%async_computation.8 | async-start | bytes 4456448 | tf_op jit(solution)/shard_map/reduce_scatter | solution.py:38
  243.1 0.9 copy-start.1
  243.1 199.0 %all-reduce.3.cloned.1.call-start = ((), (), s32[]{:S(2)}) async-start(), calls=%async_computation.9 | async-start | bytes 262144 | tf_op jit(solution)/shard_map/psum | solution.py:49
Sparse Core Ops, SparseCore 0:
  9.5 57.8 all-gather.3
  91.8 72.0 reduce-scatter.3
  166.7 40.0 all-gather.5
  208.8 14.4 reduce-scatter.5
  231.2 40.2 all-gather.7
  275.3 71.9 reduce-scatter.7
  351.4 90.6 all-reduce.2
where the time goes:
time: 453 us; the launch traced here: 452 us
  waiting for transfers between devices  355 us (78%)
  matrix products  31.6 us (7%)
  local copies, waits for them, and re-layouts  31 us (7%)
  between operations  14.2 us (3%)
  blocking collectives  11.6 us (3%)
  other arithmetic  7.83 us (2%)
    reduce_scatter x2, waiting for transfers between devices, backward_scatter(): lax.psum_scatter(summed.reshape(count, width), 'dom', scatter_dimension=0...  136 us
    psum x1, waiting for transfers between devices, weight_grad(): lax.psum(jnp.dot(full.T, back, preferred_element_type=jnp.float32).astype...  87.5 us
    all_gather x2, waiting for transfers between devices, forward_fold(): piece = lax.all_gather(prod, 'dom', axis=0, tiled=True)  67.3 us
    all_gather x1, waiting for transfers between devices, body(): all_vals = lax.all_gather(block_vals, 'col', axis=1, tiled=True)  58.8 us
    all_gather x2, blocking collectives, widen(): return lax.all_gather(value, 'col', axis=1, tiled=True)  11.6 us
    dot_general x2, matrix products, forward_fold(): jnp.einsum('rkij,rkjf->rif', vals, picked, preferred_element_type=jnp.flo...  10.4 us
  transfers between devices with their start and end apart: 7, of which 7 were waited for; matrix products, arithmetic and copies ran while one was open for 8% of the time, Pallas kernels for 0%

commit v1 on v0

--- a/solution.py
+++ b/solution.py
@@ -13,7 +13,19 @@
 
 def forward_fold(prod, cols, vals):
     rows, width = prod.shape
-    piece = lax.all_gather(prod, "dom", axis=0, tiled=True)
+    world = lax.axis_size("dom")
+    cards = tuple(((i, (i + 1) % world) for i in range(world)))
+    inbox = tuple(((i, (i - 1) % world) for i in range(world)))
+    right_arr, aux = ([prod], [prod])
+    for _ in range(world // 2):
+        right_arr.append(lax.ppermute(right_arr[-1], "dom", cards))
+    for _ in range((world - 1) // 2):
+        aux.append(lax.ppermute(aux[-1], "dom", inbox))
+    piece = jnp.roll(
+        jnp.concatenate([*right_arr[::-1], *aux[1:]], axis=0),
+        shift=(lax.axis_index("dom") - world // 2) * prod.shape[0],
+        axis=0,
+    )
     count_blocks = piece.shape[0] // BLK
     hit = (cols >= 0) & (cols < count_blocks)
     picked = piece.reshape(count_blocks, BLK, width)[jnp.clip(cols, 0, count_blocks - 1)]

time: 453 us -> 387 us (0.85)
  waiting for transfers between devices: 355 us -> 238 us
  starting transfers between devices: 0.47 us -> 40.5 us
  other arithmetic: 7.83 us -> 16.9 us
    reduce_scatter x2, waiting for transfers between devices: 136 us -> 29.1 us  [backward_scatter(): lax.psum_scatter(summed.reshape(count, width), 'dom', scatter_dimension=0...]
    all_gather x2 -> x0, waiting for transfers between devices: 67.3 us -> none  [forward_fold(): piece = lax.all_gather(prod, 'dom', axis=0, tiled=True)]
    ppermute x0 -> x30, waiting for transfers between devices: none -> 60.1 us  [the longest x16 50.4 us: forward_fold(): right_arr.append(lax.ppermute(right_arr[-1], 'dom', cards))]
    ppermute x0 -> x30, starting transfers between devices: none -> 40.1 us  [the longest x14 39.7 us: forward_fold(): aux.append(lax.ppermute(aux[-1], 'dom', inbox))]
    concatenate x0 -> x2, other arithmetic: none -> 9.71 us  [forward_fold(): jnp.roll(jnp.concatenate([*right_arr[::-1], *aux[1:]], axis=0), shift=(la...]
    unnamed x13 -> x59, local copies, waits for them, and re-layouts: 3.31 us -> 8.4 us
    reduce_scatter x1, waiting for transfers between devices: 5.31 us -> 0.46 us  [body(): lax.psum_scatter(partial_hidden, 'col', scatter_dimension=1, tiled=True)]
  transfers between devices with their start and end apart: 7 -> 35, of which waited for: 7 -> 28; matrix products, arithmetic and copies ran while one was open for 8% -> 10% of each run, Pallas kernels for 0% -> 0%
where the time goes in v1:
time: 387 us; the launch traced here: 386 us
  waiting for transfers between devices  238 us (61%)
  starting transfers between devices  40.5 us (10%)
  local copies, waits for them, and re-layouts  34.9 us (9%)
  matrix products  30.2 us (8%)
  other arithmetic  16.9 us (4%)
  between operations  14.2 us (4%)
  blocking collectives  11.6 us (3%)
    psum x1, waiting for transfers between devices, weight_grad(): lax.psum(jnp.dot(full.T, back, preferred_element_type=jnp.float32).astype...  87.8 us
    all_gather x1, waiting for transfers between devices, body(): all_vals = lax.all_gather(block_vals, 'col', axis=1, tiled=True)  59.4 us
    ppermute x16, waiting for transfers between devices, forward_fold(): right_arr.append(lax.ppermute(right_arr[-1], 'dom', cards))  50.4 us
    ppermute x14, starting transfers between devices, forward_fold(): aux.append(lax.ppermute(aux[-1], 'dom', inbox))  39.7 us
    reduce_scatter x2, waiting for transfers between devices, backward_scatter(): lax.psum_scatter(summed.reshape(count, width), 'dom', scatter_dimension=0...  29.1 us
    all_gather x2, blocking collectives, widen(): return lax.all_gather(value, 'col', axis=1, tiled=True)  11.6 us
    dot_general x2, matrix products, forward_fold(): jnp.einsum('rkij,rkjf->rif', vals, picked, preferred_element_type=jnp.flo...  10.3 us
    concatenate x2, other arithmetic, forward_fold(): jnp.roll(jnp.concatenate([*right_arr[::-1], *aux[1:]], axis=0), shift=(la...  9.71 us
  transfers between devices with their start and end apart: 35, of which 28 were waited for; matrix products, arithmetic and copies ran while one was open for 10% of the time, Pallas kernels for 0%

profile of v1, /device:TPU:8, one launch (start us, length us, event | category | flops | bytes accessed | tf_op | source)
XLA Modules:
  0.0 385.9 jit_solution(2174447159868408131)
XLA Ops:
  8.1 59.4 %all-gather.2.cloned.1.call-done = bf16[4,32,128,128]{3,2,1,0:T(8,128)(2,1)} async-done(((bf16[4,16,128,128]{3,2,1,0:T(8,128)(2,1)}), bf16[4,32,128,128]{3,2,1,0:T(8,128)(2,1)}) %all-gather.2.cloned.1.call-update) | async-done | bytes 4194320 | tf_op jit(solution)/shard_map/all_gather | solution.py:65
  67.5 4.5 %broadcast_select_fusion = bf16[4,32,128,128]{3,2,1,0:T(8,128)(2,1)} fusion(bf16[4,32,128,128]{3,2,1,0:T(8,128)(2,1)} %all-gather.2.cloned.1.call-done, pred[4,32]{1,0:T(4,128)(4,1)S(1)} %iota_compare_fusion.1), kind=kLoop, calls=%fused_computation.12 | loop fusion | flops 2097152 | bytes 8388736 | tf_op jit(solution)/shard_map/jit(_where)/select_n | solution.py:68
  72.0 8.0 %copy.17 = bf16[4,32,128,128]{2,1,0,3:T(8,128)(2,1)} copy(bf16[4,32,128,128]{3,2,1,0:T(8,128)(2,1)} %broadcast_select_fusion) | data formatting | bytes 8388608 | tf_op jit(solution)/shard_map/jit(_where)/select_n | solution.py:68
  79.9 3.4 fusion.33
  83.4 3.9 %convolution_bitcast_fusion.1 = f32[64,128,128]{2,0,1:T(8,128)S(1)} fusion(f32[4,32,128,128]{3,1,0,2:T(8,128)S(1)} %fusion.33, s32[4,32]{1,0:T(4,128)S(1)} %copy-done.12), kind=kOutput, calls=%fused_computation.14 | convolution fusion | flops 1610620928 | bytes 12583424 | tf_op jit(solution)/shard_map/rkp,rkjf->pjf/dot_general | solution.py:49
  87.3 4.5 %copy.16 = f32[64,128,128]{2,1,0:T(8,128)} copy(f32[64,128,128]{2,0,1:T(8,128)S(1)} %convolution_bitcast_fusion.1) | data formatting | bytes 8388608 | tf_op jit(solution)/shard_map/rkp,rkjf->pjf/dot_general | solution.py:49
  92.7 5.8 %all_gather.10 = bf16[512,256]{1,0:T(8,128)(2,1)S(1)} all-gather(bf16[512,128]{1,0:T(8,128)(2,1)S(1)} %copy-done.3), channel_id=1, replica_groups=mesh['dom'=16,'col'=2] {'col'}, dimensions={1}, use_global_device_ids=true | all-gather | bytes 393216 | tf_op jit(solution)/shard_map/all_gather | solution.py:58
  98.8 5.3 %collective-permute-done = bf16[512,128]{0,1:T(8,128)(2,1)S(1)} collective-permute-done((bf16[512,128]{0,1:T(8,128)(2,1)S(1)}, bf16[512,128]{0,1:T(8,128)(2,1)S(1)}, u32[]{:S(2)}, u32[]{:S(2)}) %collective-permute-start) | collective-permute-done | bytes 131104 | tf_op jit(solution)/shard_map/ppermute | solution.py:21
  104.1 2.6 collective-permute-start.8
  106.7 2.7 collective-permute-done.1
  109.5 2.6 collective-permute-start.9
  112.1 2.7 collective-permute-done.2
  114.9 2.6 collective-permute-start.10
  117.5 2.7 collective-permute-done.3
  120.3 2.6 collective-permute-start.11
  122.9 5.3 %collective-permute-done.4 = bf16[512,128]{0,1:T(8,128)(2,1)S(1)} collective-permute-done((bf16[512,128]{0,1:T(8,128)(2,1)S(1)}, bf16[512,128]{0,1:T(8,128)(2,1)S(1)}, u32[]{:S(2)}, u32[]{:S(2)}) %collective-permute-start.4) | collective-permute-done | bytes 131104 | tf_op jit(solution)/shard_map/ppermute | solution.py:21
  128.5 3.2 collective-permute-start.12
  134.9 3.3 collective-permute-start.13
  141.4 2.9 collective-permute-start.14
  144.3 3.6 collective-permute-done.7
  153.6 18.4 %reduce-scatter.4.cloned.1.call-done = f32[512,128]{1,0:T(8,128)} async-done(((f32[8192,128]{1,0:T(8,128)}), f32[512,128]{1,0:T(8,128)}) %reduce-scatter.4.cloned.1.call-update) | async-done | bytes 262160 | tf_op jit(solution)/shard_map/reduce_scatter | solution.py:50
  174.3 2.4 fusion.7
  176.7 3.2 copy.14
  179.9 3.1 gather_fusion
  183.0 4.8 %fusion.2 = f32[4,128,128,1]{2,1,3,0:T(8,128)S(1)} fusion(bf16[4,32,128,128]{3,2,1,0:T(8,128)(2,1)} %broadcast_select_fusion, bf16[4,32,128,128]{3,2,1,0:T(8,128)(2,1)} %bitcast.68, pred[4,32]{1,0:T(4,128)(4,1)S(1)} %compare_and_fusion), kind=kOutput, calls=%fused_computation.8 | convolution fusion | flops 538968064 | bytes 8650880 | tf_op jit(solution)/shard_map/rkij,rkjf->rif/dot_general | solution.py:33
  189.4 3.4 fusion.34
  192.8 3.9 %convolution_bitcast_fusion = f32[64,128,128]{2,0,1:T(8,128)S(1)} fusion(f32[4,32,128,128]{3,1,0,2:T(8,128)S(1)} %fusion.34, s32[4,32]{1,0:T(4,128)S(1)} %copy-done.12), kind=kOutput, calls=%fused_computation.13 | convolution fusion | flops 1610620928 | bytes 12583424 | tf_op jit(solution)/shard_map/rkp,rkjf->pjf/dot_general | solution.py:49
  196.8 4.5 %copy.18 = f32[64,128,128]{2,1,0:T(8,128)} copy(f32[64,128,128]{2,0,1:T(8,128)S(1)} %convolution_bitcast_fusion) | data formatting | bytes 8388608 | tf_op jit(solution)/shard_map/rkp,rkjf->pjf/dot_general | solution.py:49
  201.4 5.8 %all_gather.11 = bf16[512,256]{1,0:T(8,128)(2,1)S(1)} all-gather(bf16[512,128]{1,0:T(8,128)(2,1)S(1)} %get-tuple-element.16), channel_id=1, replica_groups=mesh['dom'=16,'col'=2] {'col'}, dimensions={1}, use_global_device_ids=true | all-gather | bytes 393216 | tf_op jit(solution)/shard_map/all_gather | solution.py:58
  207.5 5.3 %collective-permute-done.15 = bf16[512,128]{1,0:T(8,128)(2,1)S(1)} collective-permute-done((bf16[512,128]{1,0:T(8,128)(2,1)S(1)}, bf16[512,128]{1,0:T(8,128)(2,1)S(1)}, u32[]{:S(2)}, u32[]{:S(2)}) %collective-permute-start.15) | collective-permute-done | bytes 131104 | tf_op jit(solution)/shard_map/ppermute | solution.py:21
  212.7 2.6 collective-permute-start.23
  215.4 2.7 collective-permute-done.16
  218.1 2.6 collective-permute-start.24
  220.8 2.7 collective-permute-done.17
  223.5 2.6 collective-permute-start.25
  226.2 2.7 collective-permute-done.18
  228.9 2.6 collective-permute-start.26
  231.6 5.3 %collective-permute-done.19 = bf16[512,128]{1,0:T(8,128)(2,1)S(1)} collective-permute-done((bf16[512,128]{1,0:T(8,128)(2,1)S(1)}, bf16[512,128]{1,0:T(8,128)(2,1)S(1)}, u32[]{:S(2)}, u32[]{:S(2)}) %collective-permute-start.19) | collective-permute-done | bytes 131104 | tf_op jit(solution)/shard_map/ppermute | solution.py:21
  237.9 3.2 collective-permute-start.27
  244.3 2.9 collective-permute-start.28
  249.9 3.1 collective-permute-start.29
  253.0 3.1 collective-permute-done.22
  256.5 3.4 collective-permute-done.29
  259.9 7.3 %fusion.6 = bf16[8192,128]{1,0:T(8,128)(2,1)S(1)} fusion(s32[]{:T(128)S(6)} %select_n.37, bf16[8192,128]{1,0:T(8,128)(2,1)S(1)} %constant_dynamic-update-slice_fusion.16), kind=kLoop, calls=%fused_computation.15 | loop fusion | flops 4194304 | bytes 4194308 | tf_op jit(solution)/shard_map/jit(_roll_dynamic)/concatenate | solution.py:24
  267.2 3.1 gather_fusion.1
  270.3 10.7 %reduce-scatter.8.cloned.1.call-done = f32[512,128]{1,0:T(8,128)} async-done(((f32[8192,128]{1,0:T(8,128)}), f32[512,128]{1,0:T(8,128)}) %reduce-scatter.8.cloned.1.call-update) | async-done | bytes 262160 | tf_op jit(solution)/shard_map/reduce_scatter | solution.py:50
  282.9 5.5 %fusion = f32[4,128,128,1]{2,1,3,0:T(8,128)} fusion(bf16[4,32,128,128]{3,2,1,0:T(8,128)(2,1)} %broadcast_select_fusion, bf16[4,32,128,128]{3,2,1,0:T(8,128)(2,1)} %bitcast.67, pred[4,32]{1,0:T(4,128)(4,1)S(1)} %compare_and_fusion), kind=kOutput, calls=%fused_computation.6 | convolution fusion | flops 538968064 | bytes 8650880 | tf_op jit(solution)/shard_map/rkij,rkjf->rif/dot_general | solution.py:33
  288.4 87.8 %all-reduce.3.cloned.1.call-done = (bf16[256,128]{0,1:T(8,128)(2,1)}, bf16[256,128]{1,0:T(8,128)(2,1)}) async-done(((bf16[256,128]{0,1:T(8,128)(2,1)}, bf16[256,128]{1,0:T(8,128)(2,1)}), (bf16[256,128]{0,1:T(8,128)(2,1)}, bf16[256,128]{1,0:T(8,128)(2,1)})) %all-reduce.3.cloned.1.call-update) | async-done | bytes 131088 | tf_op jit(solution)/shard_map/psum | solution.py:61
  (117 shorter events, 30.7 us)
Async XLA Ops:
  7.2 72.8 %copy-start = (bf16[512,128]{1,0:T(8,128)(2,1)S(1)}, bf16[512,128]{1,0:T(8,128)(2,1)}, u32[]{:S(2)}) copy-start(bf16[512,128]{1,0:T(8,128)(2,1)} %param.15) | copy-start | bytes 393220
  7.2 60.3 %all-gather.2.cloned.1.call-start = ((), (), s32[]{:S(2)}) async-start(), calls=%async_computation.3 | async-start | bytes 6291456 | tf_op jit(solution)/shard_map/all_gather | solution.py:65
  7.9 164.1 %reduce-scatter.4.cloned.1.call-start = ((), (), s32[]{:S(2)}) async-start(), calls=%async_computation.4 | async-start | bytes 4456448 | tf_op jit(solution)/shard_map/reduce_scatter | solution.py:50
  79.9 3.4 copy-start.12
  91.8 0.9 copy-start.3
  91.8 6.7 %copy-start.11 = (bf16[256,256]{1,0:T(8,128)(2,1)S(1)}, bf16[256,256]{1,0:T(8,128)(2,1)}, u32[]{:S(2)}) copy-start(bf16[256,256]{1,0:T(8,128)(2,1)} %param.10) | copy-start | bytes 393220
  91.8 96.5 %reduce-scatter.6.cloned.1.call-start = ((), (), s32[]{:S(2)}) async-start(), calls=%async_computation.5 | async-start | bytes 786432 | tf_op jit(solution)/shard_map/reduce_scatter | solution.py:89
  98.7 5.3 %collective-permute-start = (bf16[512,128]{0,1:T(8,128)(2,1)S(1)}, bf16[512,128]{0,1:T(8,128)(2,1)S(1)}, u32[]{:S(2)}, u32[]{:S(2)}) collective-permute-start(bf16[512,128]{0,1:T(8,128)(2,1)S(1)} %fusion.10), channel_id=1, source_target_pairs={{0,2},{2,4},{4,6},{6,8},{8,10},{10,12},{12,14},{14,16},{16,18},{18... | collective-permute-start | bytes 393224 | tf_op jit(solution)/shard_map/ppermute | solution.py:21
  104.1 5.4 %collective-permute-start.1 = (bf16[512,128]{0,1:T(8,128)(2,1)S(1)}, bf16[512,128]{0,1:T(8,128)(2,1)S(1)}, u32[]{:S(2)}, u32[]{:S(2)}) collective-permute-start(bf16[512,128]{0,1:T(8,128)(2,1)S(1)} %collective-permute-done), channel_id=1, source_target_pairs={{0,2},{2,4},{4,6},{6,8},{8,10},{10,12},{12,14},{14,16},{16,18},{18... | collective-permute-start | bytes 393224 | tf_op jit(solution)/shard_map/ppermute | solution.py:21
  104.1 5.4 %collective-permute-start.8 = (bf16[512,128]{0,1:T(8,128)(2,1)S(1)}, bf16[512,128]{0,1:T(8,128)(2,1)S(1)}, u32[]{:S(2)}, u32[]{:S(2)}) collective-permute-start(bf16[512,128]{0,1:T(8,128)(2,1)S(1)} %fusion.10), channel_id=1, source_target_pairs={{0,30},{2,0},{4,2},{6,4},{8,6},{10,8},{12,10},{14,12},{16,14},{18,... | collective-permute-start | bytes 393224 | tf_op jit(solution)/shard_map/ppermute | solution.py:23
  109.5 5.4 %collective-permute-start.2 = (bf16[512,128]{0,1:T(8,128)(2,1)S(1)}, bf16[512,128]{0,1:T(8,128)(2,1)S(1)}, u32[]{:S(2)}, u32[]{:S(2)}) collective-permute-start(bf16[512,128]{0,1:T(8,128)(2,1)S(1)} %collective-permute-done.1), channel_id=1, source_target_pairs={{0,2},{2,4},{4,6},{6,8},{8,10},{10,12},{12,14},{14,16},{16,18},{18... | collective-permute-start | bytes 393224 | tf_op jit(solution)/shard_map/ppermute | solution.py:21
  109.5 5.4 %collective-permute-start.9 = (bf16[512,128]{0,1:T(8,128)(2,1)S(1)}, bf16[512,128]{0,1:T(8,128)(2,1)S(1)}, u32[]{:S(2)}, u32[]{:S(2)}) collective-permute-start(bf16[512,128]{0,1:T(8,128)(2,1)S(1)} %collective-permute-done.8), channel_id=1, source_target_pairs={{0,30},{2,0},{4,2},{6,4},{8,6},{10,8},{12,10},{14,12},{16,14},{18,... | collective-permute-start | bytes 393224 | tf_op jit(solution)/shard_map/ppermute | solution.py:23
  114.9 5.4 %collective-permute-start.3 = (bf16[512,128]{0,1:T(8,128)(2,1)S(1)}, bf16[512,128]{0,1:T(8,128)(2,1)S(1)}, u32[]{:S(2)}, u32[]{:S(2)}) collective-permute-start(bf16[512,128]{0,1:T(8,128)(2,1)S(1)} %collective-permute-done.2), channel_id=1, source_target_pairs={{0,2},{2,4},{4,6},{6,8},{8,10},{10,12},{12,14},{14,16},{16,18},{18... | collective-permute-start | bytes 393224 | tf_op jit(solution)/shard_map/ppermute | solution.py:21
  114.9 5.4 %collective-permute-start.10 = (bf16[512,128]{0,1:T(8,128)(2,1)S(1)}, bf16[512,128]{0,1:T(8,128)(2,1)S(1)}, u32[]{:S(2)}, u32[]{:S(2)}) collective-permute-start(bf16[512,128]{0,1:T(8,128)(2,1)S(1)} %collective-permute-done.9), channel_id=1, source_target_pairs={{0,30},{2,0},{4,2},{6,4},{8,6},{10,8},{12,10},{14,12},{16,14},{18,... | collective-permute-start | bytes 393224 | tf_op jit(solution)/shard_map/ppermute | solution.py:23
  120.3 19.5 %copy-start.5 = (bf16[512,128]{0,1:T(8,128)(2,1)}, bf16[512,128]{0,1:T(8,128)(2,1)S(1)}, u32[]{:S(2)}) copy-start(bf16[512,128]{0,1:T(8,128)(2,1)S(1)} %collective-permute-done.3) | copy-start | bytes 393220
  120.3 7.9 %collective-permute-start.4 = (bf16[512,128]{0,1:T(8,128)(2,1)S(1)}, bf16[512,128]{0,1:T(8,128)(2,1)S(1)}, u32[]{:S(2)}, u32[]{:S(2)}) collective-permute-start(bf16[512,128]{0,1:T(8,128)(2,1)S(1)} %collective-permute-done.3), channel_id=1, source_target_pairs={{0,2},{2,4},{4,6},{6,8},{8,10},{10,12},{12,14},{14,16},{16,18},{18... | collective-permute-start | bytes 393224 | tf_op jit(solution)/shard_map/ppermute | solution.py:21
  120.3 8.2 %collective-permute-start.11 = (bf16[512,128]{0,1:T(8,128)(2,1)S(1)}, bf16[512,128]{0,1:T(8,128)(2,1)S(1)}, u32[]{:S(2)}, u32[]{:S(2)}) collective-permute-start(bf16[512,128]{0,1:T(8,128)(2,1)S(1)} %collective-permute-done.10), channel_id=1, source_target_pairs={{0,30},{2,0},{4,2},{6,4},{8,6},{10,8},{12,10},{14,12},{16,14},{18,... | collective-permute-start | bytes 393224 | tf_op jit(solution)/shard_map/ppermute | solution.py:23
  128.2 16.1 %copy-start.8 = (bf16[512,128]{0,1:T(8,128)(2,1)}, bf16[512,128]{0,1:T(8,128)(2,1)S(1)}, u32[]{:S(2)}) copy-start(bf16[512,128]{0,1:T(8,128)(2,1)S(1)} %collective-permute-done.4) | copy-start | bytes 393220
  128.2 5.5 %collective-permute-start.5 = (bf16[512,128]{0,1:T(8,128)(2,1)S(1)}, bf16[512,128]{0,1:T(8,128)(2,1)S(1)}, u32[]{:S(2)}, u32[]{:S(2)}) collective-permute-start(bf16[512,128]{0,1:T(8,128)(2,1)S(1)} %collective-permute-done.4), channel_id=1, source_target_pairs={{0,2},{2,4},{4,6},{6,8},{8,10},{10,12},{12,14},{14,16},{16,18},{18... | collective-permute-start | bytes 393224 | tf_op jit(solution)/shard_map/ppermute | solution.py:21
  128.5 6.4 %collective-permute-start.12 = (bf16[512,128]{0,1:T(8,128)(2,1)S(1)}, bf16[512,128]{0,1:T(8,128)(2,1)S(1)}, u32[]{:S(2)}, u32[]{:S(2)}) collective-permute-start(bf16[512,128]{0,1:T(8,128)(2,1)S(1)} %collective-permute-done.11), channel_id=1, source_target_pairs={{0,30},{2,0},{4,2},{6,4},{8,6},{10,8},{12,10},{14,12},{16,14},{18,... | collective-permute-start | bytes 393224 | tf_op jit(solution)/shard_map/ppermute | solution.py:23
  133.7 10.6 %copy-start.9 = (bf16[512,128]{0,1:T(8,128)(2,1)}, bf16[512,128]{0,1:T(8,128)(2,1)S(1)}, u32[]{:S(2)}) copy-start(bf16[512,128]{0,1:T(8,128)(2,1)S(1)} %collective-permute-done.5) | copy-start | bytes 393220
  133.7 6.0 %collective-permute-start.6 = (bf16[512,128]{0,1:T(8,128)(2,1)S(1)}, bf16[512,128]{0,1:T(8,128)(2,1)S(1)}, u32[]{:S(2)}, u32[]{:S(2)}) collective-permute-start(bf16[512,128]{0,1:T(8,128)(2,1)S(1)} %collective-permute-done.5), channel_id=1, source_target_pairs={{0,2},{2,4},{4,6},{6,8},{8,10},{10,12},{12,14},{14,16},{16,18},{18... | collective-permute-start | bytes 393224 | tf_op jit(solution)/shard_map/ppermute | solution.py:21
  134.9 9.4 %copy-start.6 = (bf16[512,128]{0,1:T(8,128)(2,1)}, bf16[512,128]{0,1:T(8,128)(2,1)S(1)}, u32[]{:S(2)}) copy-start(bf16[512,128]{0,1:T(8,128)(2,1)S(1)} %collective-permute-done.12) | copy-start | bytes 393220
  134.9 6.5 %collective-permute-start.13 = (bf16[512,128]{0,1:T(8,128)(2,1)S(1)}, bf16[512,128]{0,1:T(8,128)(2,1)}, u32[]{:S(2)}, u32[]{:S(2)}) collective-permute-start(bf16[512,128]{0,1:T(8,128)(2,1)S(1)} %collective-permute-done.12), channel_id=1, source_target_pairs={{0,30},{2,0},{4,2},{6,4},{8,6},{10,8},{12,10},{14,12},{16,14},{18,... | collective-permute-start | bytes 393224 | tf_op jit(solution)/shard_map/ppermute | solution.py:23
  139.7 4.6 %copy-start.10 = (bf16[512,128]{0,1:T(8,128)(2,1)}, bf16[512,128]{0,1:T(8,128)(2,1)S(1)}, u32[]{:S(2)}) copy-start(bf16[512,128]{0,1:T(8,128)(2,1)S(1)} %collective-permute-done.6) | copy-start | bytes 393220
  139.7 8.2 %collective-permute-start.7 = (bf16[512,128]{0,1:T(8,128)(2,1)S(1)}, bf16[512,128]{0,1:T(8,128)(2,1)}, u32[]{:S(2)}, u32[]{:S(2)}) collective-permute-start(bf16[512,128]{0,1:T(8,128)(2,1)S(1)} %collective-permute-done.6), channel_id=1, source_target_pairs={{0,2},{2,4},{4,6},{6,8},{8,10},{10,12},{12,14},{14,16},{16,18},{18... | collective-permute-start | bytes 393224 | tf_op jit(solution)/shard_map/ppermute | solution.py:21
  139.8 32.2 %copy-start.4 = (bf16[256,256]{1,0:T(8,128)(2,1)S(1)}, bf16[256,256]{1,0:T(8,128)(2,1)}, u32[]{:S(2)}) copy-start(bf16[256,256]{1,0:T(8,128)(2,1)} %param.11) | copy-start | bytes 393220
  141.4 12.2 %collective-permute-start.14 = (bf16[512,128]{0,1:T(8,128)(2,1)}, bf16[512,128]{0,1:T(8,128)(2,1)S(1)}, u32[]{:S(2)}, u32[]{:S(2)}) collective-permute-start(bf16[512,128]{0,1:T(8,128)(2,1)} %collective-permute-done.13), channel_id=1, source_target_pairs={{0,30},{2,0},{4,2},{6,4},{8,6},{10,8},{12,10},{14,12},{16,14},{18,... | collective-permute-start | bytes 393224 | tf_op jit(solution)/shard_map/ppermute | solution.py:23
  147.9 4.8 %copy-start.7 = (bf16[512,128]{0,1:T(8,128)(2,1)S(1)}, bf16[512,128]{0,1:T(8,128)(2,1)}, u32[]{:S(2)}) copy-start(bf16[512,128]{0,1:T(8,128)(2,1)} %copy-done.6) | copy-start | bytes 393220
  174.0 107.1 %reduce-scatter.8.cloned.1.call-start = ((), (), s32[]{:S(2)}) async-start(), calls=%async_computation.6 | async-start | bytes 4456448 | tf_op jit(solution)/shard_map/reduce_scatter | solution.py:50
  201.3 47.3 %copy-start.2 = (f32[512,128]{1,0:T(8,128)S(1)}, f32[512,128]{1,0:T(8,128)}, u32[]{:S(2)}) copy-start(f32[512,128]{1,0:T(8,128)} %reduce-scatter.4.cloned.1.call-done) | copy-start | bytes 786436
  201.3 174.9 %all-reduce.3.cloned.1.call-start = ((), (), s32[]{:S(2)}) async-start(), calls=%async_computation.7 | async-start | bytes 262144 | tf_op jit(solution)/shard_map/psum | solution.py:61
  207.4 5.3 %collective-permute-start.15 = (bf16[512,128]{1,0:T(8,128)(2,1)S(1)}, bf16[512,128]{1,0:T(8,128)(2,1)S(1)}, u32[]{:S(2)}, u32[]{:S(2)}) collective-permute-start(bf16[512,128]{1,0:T(8,128)(2,1)S(1)} %convolution_convert_fusion), channel_id=1, source_target_pairs={{0,2},{2,4},{4,6},{6,8},{8,10},{10,12},{12,14},{14,16},{16,18},{18... | collective-permute-start | bytes 393224 | tf_op jit(solution)/shard_map/ppermute | solution.py:21
  212.7 5.4 %collective-permute-start.16 = (bf16[512,128]{1,0:T(8,128)(2,1)S(1)}, bf16[512,128]{1,0:T(8,128)(2,1)S(1)}, u32[]{:S(2)}, u32[]{:S(2)}) collective-permute-start(bf16[512,128]{1,0:T(8,128)(2,1)S(1)} %collective-permute-done.15), channel_id=1, source_target_pairs={{0,2},{2,4},{4,6},{6,8},{8,10},{10,12},{12,14},{14,16},{16,18},{18... | collective-permute-start | bytes 393224 | tf_op jit(solution)/shard_map/ppermute | solution.py:21
  212.7 5.4 %collective-permute-start.23 = (bf16[512,128]{1,0:T(8,128)(2,1)S(1)}, bf16[512,128]{1,0:T(8,128)(2,1)S(1)}, u32[]{:S(2)}, u32[]{:S(2)}) collective-permute-start(bf16[512,128]{1,0:T(8,128)(2,1)S(1)} %convolution_convert_fusion), channel_id=1, source_target_pairs={{0,30},{2,0},{4,2},{6,4},{8,6},{10,8},{12,10},{14,12},{16,14},{18,... | collective-permute-start | bytes 393224 | tf_op jit(solution)/shard_map/ppermute | solution.py:23
  218.1 5.4 %collective-permute-start.17 = (bf16[512,128]{1,0:T(8,128)(2,1)S(1)}, bf16[512,128]{1,0:T(8,128)(2,1)S(1)}, u32[]{:S(2)}, u32[]{:S(2)}) collective-permute-start(bf16[512,128]{1,0:T(8,128)(2,1)S(1)} %collective-permute-done.16), channel_id=1, source_target_pairs={{0,2},{2,4},{4,6},{6,8},{8,10},{10,12},{12,14},{14,16},{16,18},{18... | collective-permute-start | bytes 393224 | tf_op jit(solution)/shard_map/ppermute | solution.py:21
  218.1 5.4 %collective-permute-start.24 = (bf16[512,128]{1,0:T(8,128)(2,1)S(1)}, bf16[512,128]{1,0:T(8,128)(2,1)S(1)}, u32[]{:S(2)}, u32[]{:S(2)}) collective-permute-start(bf16[512,128]{1,0:T(8,128)(2,1)S(1)} %collective-permute-done.23), channel_id=1, source_target_pairs={{0,30},{2,0},{4,2},{6,4},{8,6},{10,8},{12,10},{14,12},{16,14},{18,... | collective-permute-start | bytes 393224 | tf_op jit(solution)/shard_map/ppermute | solution.py:23
  223.5 5.4 %collective-permute-start.18 = (bf16[512,128]{1,0:T(8,128)(2,1)S(1)}, bf16[512,128]{1,0:T(8,128)(2,1)S(1)}, u32[]{:S(2)}, u32[]{:S(2)}) collective-permute-start(bf16[512,128]{1,0:T(8,128)(2,1)S(1)} %collective-permute-done.17), channel_id=1, source_target_pairs={{0,2},{2,4},{4,6},{6,8},{8,10},{10,12},{12,14},{14,16},{16,18},{18... | collective-permute-start | bytes 393224 | tf_op jit(solution)/shard_map/ppermute | solution.py:21
  223.5 5.4 %collective-permute-start.25 = (bf16[512,128]{1,0:T(8,128)(2,1)S(1)}, bf16[512,128]{1,0:T(8,128)(2,1)S(1)}, u32[]{:S(2)}, u32[]{:S(2)}) collective-permute-start(bf16[512,128]{1,0:T(8,128)(2,1)S(1)} %collective-permute-done.24), channel_id=1, source_target_pairs={{0,30},{2,0},{4,2},{6,4},{8,6},{10,8},{12,10},{14,12},{16,14},{18,... | collective-permute-start | bytes 393224 | tf_op jit(solution)/shard_map/ppermute | solution.py:23
  228.9 8.0 %collective-permute-start.19 = (bf16[512,128]{1,0:T(8,128)(2,1)S(1)}, bf16[512,128]{1,0:T(8,128)(2,1)S(1)}, u32[]{:S(2)}, u32[]{:S(2)}) collective-permute-start(bf16[512,128]{1,0:T(8,128)(2,1)S(1)} %collective-permute-done.18), channel_id=1, source_target_pairs={{0,2},{2,4},{4,6},{6,8},{8,10},{10,12},{12,14},{14,16},{16,18},{18... | collective-permute-start | bytes 393224 | tf_op jit(solution)/shard_map/ppermute | solution.py:21
  228.9 9.0 %collective-permute-start.26 = (bf16[512,128]{1,0:T(8,128)(2,1)S(1)}, bf16[512,128]{1,0:T(8,128)(2,1)S(1)}, u32[]{:S(2)}, u32[]{:S(2)}) collective-permute-start(bf16[512,128]{1,0:T(8,128)(2,1)S(1)} %collective-permute-done.25), channel_id=1, source_target_pairs={{0,30},{2,0},{4,2},{6,4},{8,6},{10,8},{12,10},{14,12},{16,14},{18,... | collective-permute-start | bytes 393224 | tf_op jit(solution)/shard_map/ppermute | solution.py:23
  236.9 5.7 %collective-permute-start.20 = (bf16[512,128]{1,0:T(8,128)(2,1)S(1)}, bf16[512,128]{1,0:T(8,128)(2,1)S(1)}, u32[]{:S(2)}, u32[]{:S(2)}) collective-permute-start(bf16[512,128]{1,0:T(8,128)(2,1)S(1)} %collective-permute-done.19), channel_id=1, source_target_pairs={{0,2},{2,4},{4,6},{6,8},{8,10},{10,12},{12,14},{14,16},{16,18},{18... | collective-permute-start | bytes 393224 | tf_op jit(solution)/shard_map/ppermute | solution.py:21
  237.9 6.4 %collective-permute-start.27 = (bf16[512,128]{1,0:T(8,128)(2,1)S(1)}, bf16[512,128]{1,0:T(8,128)(2,1)S(1)}, u32[]{:S(2)}, u32[]{:S(2)}) collective-permute-start(bf16[512,128]{1,0:T(8,128)(2,1)S(1)} %collective-permute-done.26), channel_id=1, source_target_pairs={{0,30},{2,0},{4,2},{6,4},{8,6},{10,8},{12,10},{14,12},{16,14},{18,... | collective-permute-start | bytes 393224 | tf_op jit(solution)/shard_map/ppermute | solution.py:23
  242.6 5.7 %collective-permute-start.21 = (bf16[512,128]{1,0:T(8,128)(2,1)S(1)}, bf16[512,128]{1,0:T(8,128)(2,1)S(1)}, u32[]{:S(2)}, u32[]{:S(2)}) collective-permute-start(bf16[512,128]{1,0:T(8,128)(2,1)S(1)} %collective-permute-done.20), channel_id=1, source_target_pairs={{0,2},{2,4},{4,6},{6,8},{8,10},{10,12},{12,14},{14,16},{16,18},{18... | collective-permute-start | bytes 393224 | tf_op jit(solution)/shard_map/ppermute | solution.py:21
  244.3 5.6 %collective-permute-start.28 = (bf16[512,128]{1,0:T(8,128)(2,1)S(1)}, bf16[512,128]{1,0:T(8,128)(2,1)S(1)}, u32[]{:S(2)}, u32[]{:S(2)}) collective-permute-start(bf16[512,128]{1,0:T(8,128)(2,1)S(1)} %collective-permute-done.27), channel_id=1, source_target_pairs={{0,30},{2,0},{4,2},{6,4},{8,6},{10,8},{12,10},{14,12},{16,14},{18,... | collective-permute-start | bytes 393224 | tf_op jit(solution)/shard_map/ppermute | solution.py:23
  248.3 7.8 %collective-permute-start.22 = (bf16[512,128]{1,0:T(8,128)(2,1)S(1)}, bf16[512,128]{1,0:T(8,128)(2,1)S(1)}, u32[]{:S(2)}, u32[]{:S(2)}) collective-permute-start(bf16[512,128]{1,0:T(8,128)(2,1)S(1)} %collective-permute-done.21), channel_id=1, source_target_pairs={{0,2},{2,4},{4,6},{6,8},{8,10},{10,12},{12,14},{14,16},{16,18},{18... | collective-permute-start | bytes 393224 | tf_op jit(solution)/shard_map/ppermute | solution.py:21
  249.9 10.0 %collective-permute-start.29 = (bf16[512,128]{1,0:T(8,128)(2,1)S(1)}, bf16[512,128]{1,0:T(8,128)(2,1)S(1)}, u32[]{:S(2)}, u32[]{:S(2)}) collective-permute-start(bf16[512,128]{1,0:T(8,128)(2,1)S(1)} %collective-permute-done.28), channel_id=1, source_target_pairs={{0,30},{2,0},{4,2},{6,4},{8,6},{10,8},{12,10},{14,12},{16,14},{18,... | collective-permute-start | bytes 393224 | tf_op jit(solution)/shard_map/ppermute | solution.py:23
  282.9 96.4 %copy-start.1 = (bf16[512,128]{1,0:T(8,128)(2,1)S(1)}, bf16[512,128]{1,0:T(8,128)(2,1)}, u32[]{:S(2)}) copy-start(bf16[512,128]{1,0:T(8,128)(2,1)} %param.15) | copy-start | bytes 393220
  (1 other events, 0.8 us)
Sparse Core Ops, SparseCore 0:
  9.5 57.8 all-gather.1
  92.0 80.0 reduce-scatter.3
  174.2 14.0 reduce-scatter.5
  201.4 79.6 reduce-scatter.7
  285.0 91.1 all-reduce.2
